TPU v7x, 256 devices: a whole 4x4x8 slice. The times are simulated.
256 devices in a mesh: chan: 128 (over z, y, x_lo, core), stn: 2 (over x_hi).
Axes of the slice: x: 4 (x_hi: 2, x_lo: 2; x = x_hi * 2 + x_lo), y: 4, z: 8, core: 2. Of those that a mesh axis runs over, the one named last changes fastest.
Arguments:
- voltages: bfloat16 [2, 1536, 2, 256, 512], P(None, 'chan', None, None, 'stn'), may hold values from -6 to 6
- delay_table: float32 [4096], replicated, may hold values from -8 to 8
- delay_index: int32 [64, 512], P(None, 'stn'), may hold values from 0 to 4094
- delay_fraction: int32 [64, 512], P(None, 'stn'), may hold values from 0 to 65535
- station_subarray: int32 [512], P('stn'), may hold values from 0 to 3
Outputs:
- beams: bfloat16 [2, 64, 2, 256, 1536], P(None, 'stn', None, 'chan')
All inputs are finite; a program needn't handle non-finite values.
Results may differ from a plain program's by a relative error of at most 0.0068.
Values may be sent and summed in bfloat16 or wider, within the bound.
A program may use at most 128 MiB of HBM per device.

v0:
```python
import math
import jax
import jax.numpy as jnp
from jax import lax
from jax.sharding import Mesh
from jax.sharding import PartitionSpec as P

STATIONS = 512
POL = 2
NFFT = 256
TAPS = 12
GROUPS = 4
CHAN = ("chan_0", "chan_1", "chan_2", "chan_3")


def joined_along(parts, dim):
    shape = list(parts.shape[1:])
    shape[dim] *= parts.shape[0]
    return jnp.moveaxis(parts, 0, dim).reshape(shape)


def all_blocks(x, axes, turns):
    parts = x[None]
    for k in turns:
        parts = lax.all_gather(parts, axes[k], axis=0, tiled=True)
    held = [lax.axis_size(axes[k]) for k in reversed(turns)]
    parts = parts.reshape(*held, *x.shape)
    turned = sorted(range(len(turns)), key=lambda place: turns[len(turns) - 1 - place])
    return parts.transpose(*turned, *range(len(turns), parts.ndim)).reshape(-1, *x.shape)


def gather_axes(x, axes, turns, dim):
    return joined_along(all_blocks(x, axes, turns), dim)


def passed_along(value, axis, steps):
    count = lax.axis_size(axis)
    initial, last = (max(0, -steps), min(count, count - steps))
    return lax.ppermute(value, axis, [(source, source + steps) for source in range(initial, last)])


def in_blocks(x, dim, peers):
    shape = x.shape
    parts = x.reshape(*shape[:dim], peers, shape[dim] // peers, *shape[dim + 1 :])
    return jnp.moveaxis(parts, dim, 0)


def sent_and_summed(x, axis, dim):
    parts = in_blocks(x, dim, lax.axis_size(axis))
    arrived = lax.all_to_all(parts, axis, split_axis=0, concat_axis=0, tiled=True)
    return arrived.sum(axis=0)


def prototype(tap_count, points):
    length = tap_count * points
    sample_ids = jnp.arange(length, dtype=jnp.float32)
    centred = (sample_ids - (length - 1) / 2.0) / points
    window = 0.5 - 0.5 * jnp.cos(2.0 * math.pi * (sample_ids + 0.5) / length)
    coeffs = jnp.sinc(centred) * window
    coeffs = coeffs * jnp.sqrt(points / jnp.sum(coeffs * coeffs))
    return coeffs.reshape(tap_count, points)


def dft_table(points):
    indices = jnp.arange(points, dtype=jnp.int32)
    product = indices[:, None] * indices[None, :] % points
    angles = 2.0 * math.pi / points * product.astype(jnp.float32)
    cosine = jnp.cos(angles) / math.sqrt(points)
    sine_part = jnp.sin(angles) / math.sqrt(points)
    real_input = jnp.stack([cosine, -sine_part], axis=1)
    imag_input = jnp.stack([sine_part, cosine], axis=1)
    return jnp.stack([real_input, imag_input], axis=0).astype(jnp.bfloat16)


def polyphase(padded, coeffs, frame_count):
    summed = jnp.zeros(padded.shape[:1] + (frame_count,) + padded.shape[2:], jnp.float32)
    for tap_index in range(coeffs.shape[0]):
        summed = summed + coeffs[tap_index][:, None] * padded[
            :, tap_index : tap_index + frame_count
        ].astype(jnp.float32)
    return summed.astype(jnp.bfloat16)


def steering(delays, station_subarray, channel_ids):
    beam_ids = jnp.arange(delays.shape[0], dtype=jnp.int32)
    member = (station_subarray[None, :] == (beam_ids % GROUPS)[:, None]).astype(
        jnp.float32
    ) * math.sqrt(GROUPS / STATIONS)
    signed = (channel_ids + NFFT // 2) % NFFT - NFFT // 2
    frequency = signed.astype(jnp.float32) / NFFT
    phases = -2.0 * math.pi * frequency[:, None, None] * delays[None, :, :]
    real_weight = (member * jnp.cos(phases)).astype(jnp.bfloat16)
    imag_weight = (member * jnp.sin(phases)).astype(jnp.bfloat16)
    first_row = jnp.stack([real_weight, -imag_weight], axis=2)
    second_row = jnp.stack([imag_weight, real_weight], axis=2)
    return jnp.stack([first_row, second_row], axis=1)


def shards(voltages, delay_table, delay_index, delay_fraction, station_subarray):
    frames_dev = voltages.shape[1]
    local_stations = voltages.shape[4]
    beam_count = delay_index.shape[0]
    groups_chan = lax.axis_size(CHAN)
    per_dev = NFFT // groups_chan
    share = beam_count * local_stations // groups_chan
    first_entry = lax.axis_index(CHAN) * share
    index_share = lax.dynamic_slice_in_dim(delay_index.reshape(-1), first_entry, share, 0)
    fraction_share = lax.dynamic_slice_in_dim(delay_fraction.reshape(-1), first_entry, share, 0)
    lower_delay = jnp.take(delay_table, index_share, axis=0)
    upper_delay = jnp.take(delay_table, index_share + 1, axis=0)
    delay_share = lower_delay + fraction_share.astype(jnp.float32) * (1.0 / 65536.0) * (
        upper_delay - lower_delay
    )
    delays = gather_axes(delay_share, CHAN, (2, 0, 1, 3), 0).reshape(beam_count, local_stations)
    coeffs = prototype(TAPS, NFFT)
    history = passed_along(voltages[:, frames_dev - (TAPS - 1) :], CHAN, 1)
    filtered = polyphase(jnp.concatenate([history, voltages], axis=1), coeffs, frames_dev)
    dft_full = dft_table(NFFT)
    spectra = lax.dot_general(
        dft_full, filtered, (((0, 1), (2, 3)), ((), ())), preferred_element_type=jnp.float32
    ).astype(jnp.bfloat16)
    channel_ids = lax.axis_index(CHAN) * per_dev + jnp.arange(per_dev, dtype=jnp.int32)
    weights = steering(delays, station_subarray, channel_ids)
    spectra = spectra.reshape(2, groups_chan, per_dev, POL, frames_dev, local_stations)
    partial_value = lax.dot_general(
        weights,
        lax.all_to_all(spectra, CHAN, split_axis=1, concat_axis=1, tiled=True),
        (((3, 4), (0, 5)), ((0,), (2,))),
        preferred_element_type=jnp.float32,
    )
    summed = sent_and_summed(partial_value, "stn", 2).astype(jnp.bfloat16)
    ordered = jnp.transpose(summed, (1, 2, 4, 0, 3, 5))
    return ordered.reshape(2, summed.shape[2], POL, per_dev, groups_chan * frames_dev)


def solution(mesh):
    torus = Mesh(
        mesh.devices.reshape(8, 4, 2, 2, mesh.shape["stn"]),
        ("chan_0", "chan_1", "chan_2", "chan_3", "stn"),
    )
    placed = (P(None, CHAN, None, None, "stn"), P(), P(None, "stn"), P(None, "stn"), P("stn"))
    return jax.shard_map(
        shards,
        mesh=torus,
        in_specs=placed,
        out_specs=P(None, "stn", None, CHAN, None),
        check_vma=False,
    )
```

profile of v0, /device:TPU:1, one launch (start us, length us, event | category | flops | bytes accessed | tf_op | source)
XLA Modules:
  0.0 368.8 jit_solution(15485896743960134796)
XLA Ops:
  0.0 0.0 copy-start
  0.0 0.0 slice-start
  0.0 5.9 %slice.85 = bf16[2,11,2,256,256]{4,3,2,1,0:T(8,128)(2,1)} slice(bf16[2,12,2,256,256]{4,3,2,1,0:T(8,128)(2,1)} %param.7), slice={[0:2], [1:12], [0:2], [0:256], [0:256]} | slice | bytes 11534336 | tf_op jit(solution)/shard_map/slice | solution.py:116
  5.9 4.5 %collective-permute-start = (bf16[2,11,2,256,256]{4,3,2,1,0:T(8,128)(2,1)}, bf16[2,11,2,256,256]{4,3,2,1,0:T(8,128)(2,1)}, u32[]{:S(2)}, u32[]{:S(2)}) collective-permute-start(bf16[2,11,2,256,256]{4,3,2,1,0:T(8,128)(2,1)} %slice.85), channel_id=1, source_target_pairs={{0,2},{2,4},{4,6},{6,8},{8,10},{10,12},{12,14},{14,16},{16,18},{18... | collective-permute-start | bytes 17301512 | tf_op jit(solution)/shard_map/ppermute | solution.py:39
  10.4 0.7 multiply_reduce_fusion
  11.8 0.1 broadcast_multiply_fusion
  11.9 1.0 fusion.16
  12.9 1.1 negate_convert_fusion
  14.0 0.0 slice-start.1
  14.1 58.9 %collective-permute-done = bf16[2,11,2,256,256]{4,3,2,1,0:T(8,128)(2,1)} collective-permute-done((bf16[2,11,2,256,256]{4,3,2,1,0:T(8,128)(2,1)}, bf16[2,11,2,256,256]{4,3,2,1,0:T(8,128)(2,1)}, u32[]{:S(2)}, u32[]{:S(2)}) %collective-permute-start) | collective-permute-done | bytes 5767200 | tf_op jit(solution)/shard_map/ppermute | solution.py:39
  73.0 5.8 %constant_dynamic-update-slice_fusion.1 = bf16[2,23,2,256,256]{4,3,2,1,0:T(8,128)(2,1)} fusion(bf16[2,11,2,256,256]{4,3,2,1,0:T(8,128)(2,1)} %collective-permute-done), kind=kLoop, calls=%fused_computation.83 | loop fusion | bytes 11534336
  78.8 0.0 slice-done
  78.8 0.0 slice-done.1
  78.8 3.1 constant_dynamic-update-slice_fusion
  81.9 31.7 %bitcast_convert_fusion = bf16[2,256,2,12,256]{4,1,3,2,0:T(8,128)(2,1)} fusion(bf16[2,12,2,256,256]{4,3,2,1,0:T(8,128)(2,1)S(1)} %bitcast.60, f32[256]{0:T(256)S(1)} %get-tuple-element.15, bf16[2,23,2,256,256]{4,3,2,1,0:T(8,128)(2,1)} %constant_dynamic-update-slice_fusion, f32[256]{0:T(256)S(1)} %get-tuple-element.16, f32[256]{0:T(256)S(1)} %get-tuple-element.17, ...), kind=kOutput, calls=%fused_computation.2 | convolution fusion | flops 3338665984 | bytes 82325504 | tf_op jit(solution)/shard_map/dot_general | solution.py:119
  113.6 0.0 copy-start.1
  113.6 0.0 copy-start.2
  113.6 0.0 copy-start.3
  113.6 12.8 %copy.29 = bf16[2,256,2,12,256]{4,0,3,2,1:T(2,128)(2,1)} copy(bf16[2,256,2,12,256]{4,1,3,2,0:T(8,128)(2,1)} %bitcast_convert_fusion) | data formatting | bytes 12582912 | tf_op jit(solution)/shard_map/reshape | solution.py:124
  126.4 15.8 %all-to-all-start = ((bf16[2,128,2,2,12,256]{5,0,4,3,2,1:T(2,128)(2,1)}), bf16[2,128,2,2,12,256]{5,0,4,3,2,1:T(2,128)(2,1)}, u32[]{:S(2)}, u32[]{:S(2)}) async-start(bf16[2,128,2,2,12,256]{5,0,4,3,2,1:T(2,128)(2,1)} %bitcast.58), calls=%async_computation | async-start | bytes 12582912 | tf_op jit(solution)/shard_map/all_to_all | solution.py:127
  142.2 0.0 copy-done.1
  142.3 0.0 copy-done.2
  142.3 0.1 compare_select_fusion.2
  142.4 0.0 copy-done
  142.4 1.1 gather_fusion.1
  143.6 1.1 gather_fusion
  144.7 0.1 add_bitcast_fusion
  144.8 12.8 %all-gather.1 = f32[2,1,128]{2,1,0:T(1,128)S(1)} all-gather(f32[1,1,128]{2,1,0:T(1,128)S(1)} %add_bitcast_fusion), channel_id=2, replica_groups=mesh['chan_0'=8,'chan_1'=4,'chan_2'=2,'chan_3'=2,'stn'=2] {'chan_2'}, dimensions={0}, use_global_device_ids=true | all-gather | bytes 1536 | tf_op jit(solution)/shard_map/all_gather | solution.py:25
  157.6 128.6 %all-gather.2 = f32[8,2,128]{2,1,0:T(2,128)S(1)} all-gather(f32[1,2,128]{2,1,0:T(2,128)S(1)} %bitcast.75), channel_id=1, replica_groups=mesh['chan_0'=8,'chan_1'=4,'chan_2'=2,'chan_3'=2,'stn'=2] {'chan_0'}, dimensions={0}, use_global_device_ids=true | all-gather | bytes 9216 | tf_op jit(solution)/shard_map/all_gather | solution.py:25
  286.3 9.0 %all_gather.14 = f32[64,128]{1,0:T(8,128)S(1)} all-gather(f32[16,128]{1,0:T(8,128)S(1)} %bitcast.74), channel_id=1, replica_groups=mesh['chan_0'=8,'chan_1'=4,'chan_2'=2,'chan_3'=2,'stn'=2] {'chan_1'}, dimensions={0}, use_global_device_ids=true | all-gather | bytes 40960 | tf_op jit(solution)/shard_map/all_gather | solution.py:25
  295.3 7.9 %all_gather.15 = f32[128,128]{1,0:T(8,128)S(1)} all-gather(f32[64,128]{1,0:T(8,128)S(1)} %all_gather.14), channel_id=1, replica_groups=mesh['chan_0'=8,'chan_1'=4,'chan_2'=2,'chan_3'=2,'stn'=2] {'chan_3'}, dimensions={0}, use_global_device_ids=true | all-gather | bytes 98304 | tf_op jit(solution)/shard_map/all_gather | solution.py:25
  303.2 0.1 copy.15
  303.3 0.0 copy-done.3
  303.3 0.1 compare_select_fusion
  303.4 0.5 fusion.18
  303.9 0.5 fusion.57
  304.4 0.0 all-to-all-done
  304.5 10.0 %fusion = f32[2,2,64,128,2,12,1]{3,2,6,5,4,1,0:T(8,128)S(1)} fusion(bf16[2,128,2,2,12,256,1]{5,0,4,3,2,1,6:T(2,128)(2,1)} %bitcast.19, bf16[2,1,64,2,256]{4,2,3,1,0:T(8,128)(2,1)S(1)} %get-tuple-element.11, bf16[2,1,64,2,256]{4,2,3,1,0:T(8,128)(2,1)S(1)} %get-tuple-element.10), kind=kOutput, calls=%fused_computation.4 | convolution fusion | flops 805830656 | bytes 9699328 | tf_op jit(solution)/shard_map/dot_general | solution.py:125
  314.5 0.4 copy.40
  314.9 40.8 %all_to_all.10 = f32[2,2,2,32,128,2,12]{4,3,6,5,2,1,0:T(8,128)S(1)} all-to-all(f32[2,2,2,32,128,2,12]{4,3,6,5,2,1,0:T(8,128)S(1)} %bitcast.61), channel_id=1, replica_groups=mesh['chan_0'=8,'chan_1'=4,'chan_2'=2,'chan_3'=2,'stn'=2] {'stn'}, dimensions={0} | all-to-all | bytes 6291456 | tf_op jit(solution)/shard_map/all_to_all | solution.py:50
  355.7 1.4 reduce_sum.19
  357.1 6.6 %copy.22 = bf16[2,32,2,2,128,12]{1,3,5,4,2,0:T(2,128)(2,1)S(1)} copy(bf16[2,32,2,2,128,12]{4,1,5,2,0,3:T(8,128)(2,1)} %bitcast.64) | data formatting | bytes 1572864 | tf_op jit(solution)/shard_map/convert_element_type | solution.py:131
  363.8 5.0 %copy.23 = bf16[2,32,2,2,1536]{4,3,2,1,0:T(2,128)(2,1)} copy(bf16[2,32,2,2,1536]{1,3,4,2,0:T(2,128)(2,1)S(1)} %bitcast.63) | data formatting | bytes 1572864 | tf_op jit(solution)/shard_map/reshape | solution.py:133
  (10 shorter events, 0.2 us)
Async XLA Ops:
  0.0 142.4 %copy-start = (f32[4096]{0:T(1024)S(1)}, f32[4096]{0:T(1024)}, u32[]{:S(2)}) copy-start(f32[4096]{0:T(1024)} %param.8) | copy-start | bytes 49156
  0.0 78.8 %slice-start = ((s8[6291456]{0:T(1024)(128)(4,1)}), s8[2097152]{0:T(1024)(128)(4,1)S(1)}, s32[]{:S(2)}) async-start(s8[6291456]{0:T(1024)(128)(4,1)} %bitcast.59), calls=%async_computation.2 | async-start | bytes 4194304
  5.9 67.1 %collective-permute-start = (bf16[2,11,2,256,256]{4,3,2,1,0:T(8,128)(2,1)}, bf16[2,11,2,256,256]{4,3,2,1,0:T(8,128)(2,1)}, u32[]{:S(2)}, u32[]{:S(2)}) collective-permute-start(bf16[2,11,2,256,256]{4,3,2,1,0:T(8,128)(2,1)} %slice.85), channel_id=1, source_target_pairs={{0,2},{2,4},{4,6},{6,8},{8,10},{10,12},{12,14},{14,16},{16,18},{18... | collective-permute-start | bytes 17301512 | tf_op jit(solution)/shard_map/ppermute | solution.py:39
  14.0 64.8 %slice-start.1 = ((s8[6291456]{0:T(1024)(128)(4,1)}), s8[4194304]{0:T(1024)(128)(4,1)S(1)}, s32[]{:S(2)}) async-start(s8[6291456]{0:T(1024)(128)(4,1)} %bitcast.59), calls=%async_computation.3 | async-start | bytes 8388608
  113.6 28.6 %copy-start.1 = (s32[64,256]{1,0:T(8,128)S(1)}, s32[64,256]{1,0:T(8,128)}, u32[]{:S(2)}) copy-start(s32[64,256]{1,0:T(8,128)} %param.10) | copy-start | bytes 196612
  113.6 28.7 %copy-start.2 = (s32[64,256]{1,0:T(8,128)S(1)}, s32[64,256]{1,0:T(8,128)}, u32[]{:S(2)}) copy-start(s32[64,256]{1,0:T(8,128)} %param.9) | copy-start | bytes 196612
  113.6 189.7 %copy-start.3 = (s32[256]{0:T(256)S(1)}, s32[256]{0:T(256)}, u32[]{:S(2)}) copy-start(s32[256]{0:T(256)} %param.11) | copy-start | bytes 3076
  126.4 178.0 %all-to-all-start = ((bf16[2,128,2,2,12,256]{5,0,4,3,2,1:T(2,128)(2,1)}), bf16[2,128,2,2,12,256]{5,0,4,3,2,1:T(2,128)(2,1)}, u32[]{:S(2)}, u32[]{:S(2)}) async-start(bf16[2,128,2,2,12,256]{5,0,4,3,2,1:T(2,128)(2,1)} %bitcast.58), calls=%async_computation | async-start | bytes 12582912 | tf_op jit(solution)/shard_map/all_to_all | solution.py:127
where the time goes:
time: 369 us
  blocking collectives  199 us (54%)
  waiting for transfers between devices  58.9 us (16%)
  local copies, waits for them, and re-layouts  42.1 us (11%)
  matrix products  41.7 us (11%)
  starting transfers between devices  20.3 us (6%)
  other arithmetic  5.62 us (2%)
    all_gather x4, blocking collectives, all_blocks(): parts = lax.all_gather(parts, axes[k], axis=0, tiled=True)  158 us
    ppermute x1, waiting for transfers between devices, passed_along(): lax.ppermute(value, axis, [(source, source + steps) for source in range(i...  58.9 us
    all_to_all x1, blocking collectives, sent_and_summed(): lax.all_to_all(parts, axis, split_axis=0, concat_axis=0, tiled=True)  40.8 us
    dot_general x1, matrix products, shards(): lax.dot_general(dft_full, filtered, (((0, 1), (2, 3)), ((), ())), preferr...  31.7 us
    all_to_all x1, starting transfers between devices, shards(): lax.all_to_all(spectra, CHAN, split_axis=1, concat_axis=1, tiled=True)  15.8 us
    reshape x1, local copies, waits for them, and re-layouts, shards(): spectra.reshape(2, groups_chan, per_dev, POL, frames_dev, local_stations)  12.8 us
    dot_general x1, matrix products, shards(): lax.dot_general(weights, lax.all_to_all(spectra, CHAN, split_axis=1, conc...  10 us
  transfers between devices with their start and end apart: 2, of which 1 were waited for; matrix products, arithmetic and copies ran while one was open for 2% of the time, Pallas kernels for 0%

commit v1 on v0

--- a/solution.py
+++ b/solution.py
@@ -22,7 +22,9 @@
 def all_blocks(x, axes, turns):
     parts = x[None]
     for k in turns:
-        parts = lax.all_gather(parts, axes[k], axis=0, tiled=True)
+        parts = jnp.concatenate(
+            lax.all_to_all(jnp.stack([parts] * lax.axis_size(axes[k])), axes[k], 0, 0), axis=0
+        )
     held = [lax.axis_size(axes[k]) for k in reversed(turns)]
     parts = parts.reshape(*held, *x.shape)
     turned = sorted(range(len(turns)), key=lambda place: turns[len(turns) - 1 - place])

time: 369 us -> 367 us (level)
  blocking collectives: 199 us -> 39 us
  waiting for transfers between devices: 58.9 us -> 200 us
  starting transfers between devices: 20.3 us -> 30 us
    all_gather x4 -> x0, blocking collectives: 158 us -> none  [all_blocks(): parts = lax.all_gather(parts, axes[k], axis=0, tiled=True)]
    all_to_all x1, waiting for transfers between devices: 0.01 us -> 137 us  [shards(): lax.all_to_all(spectra, CHAN, split_axis=1, concat_axis=1, tiled=True)]
    all_to_all x0 -> x4, waiting for transfers between devices: none -> 63.6 us  [all_blocks(): lax.all_to_all(jnp.stack([parts] * lax.axis_size(axes[k])), axes[k], 0, 0)]
    ppermute x1, waiting for transfers between devices: 58.9 us -> 0.01 us  [passed_along(): lax.ppermute(value, axis, [(source, source + steps) for source in range(i...]
    all_to_all x0 -> x4, starting transfers between devices: none -> 18.7 us  [all_blocks(): lax.all_to_all(jnp.stack([parts] * lax.axis_size(axes[k])), axes[k], 0, 0)]
    all_to_all x1, starting transfers between devices: 15.8 us -> 6.69 us  [shards(): lax.all_to_all(spectra, CHAN, split_axis=1, concat_axis=1, tiled=True)]
    unnamed x16 -> x12, local copies, waits for them, and re-layouts: 5.88 us -> 7.69 us
  transfers between devices with their start and end apart: 2 -> 6, of which waited for: 1 -> 4; matrix products, arithmetic and copies ran while one was open for 2% -> 18% of each run, Pallas kernels for 0% -> 0%
where the time goes in v1:
time: 367 us; the launch traced here: 364 us
  waiting for transfers between devices  200 us (54%)
  local copies, waits for them, and re-layouts  45 us (12%)
  matrix products  41.7 us (11%)
  blocking collectives  39 us (11%)
  starting transfers between devices  30 us (8%)
  other arithmetic  6.9 us (2%)
    all_to_all x1, waiting for transfers between devices, shards(): lax.all_to_all(spectra, CHAN, split_axis=1, concat_axis=1, tiled=True)  137 us
    all_to_all x4, waiting for transfers between devices, all_blocks(): lax.all_to_all(jnp.stack([parts] * lax.axis_size(axes[k])), axes[k], 0, 0)  63.6 us
    all_to_all x1, blocking collectives, sent_and_summed(): lax.all_to_all(parts, axis, split_axis=0, concat_axis=0, tiled=True)  39 us
    dot_general x1, matrix products, shards(): lax.dot_general(dft_full, filtered, (((0, 1), (2, 3)), ((), ())), preferr...  31.7 us
    all_to_all x4, starting transfers between devices, all_blocks(): lax.all_to_all(jnp.stack([parts] * lax.axis_size(axes[k])), axes[k], 0, 0)  18.7 us
    reshape x1, local copies, waits for them, and re-layouts, shards(): spectra.reshape(2, groups_chan, per_dev, POL, frames_dev, local_stations)  12.8 us
    dot_general x1, matrix products, shards(): lax.dot_general(weights, lax.all_to_all(spectra, CHAN, split_axis=1, conc...  10 us
    unnamed x12, local copies, waits for them, and re-layouts  7.69 us
  transfers between devices with their start and end apart: 6, of which 4 were waited for; matrix products, arithmetic and copies ran while one was open for 18% of the time, Pallas kernels for 0%

profile of v1, /device:TPU:1, one launch (start us, length us, event | category | flops | bytes accessed | tf_op | source)
XLA Modules:
  0.0 363.8 jit_solution(14613273201415638754)
XLA Ops:
  0.0 0.0 copy-start
  0.0 5.8 %slice.85 = bf16[2,11,2,256,256]{4,3,2,1,0:T(8,128)(2,1)} slice(bf16[2,12,2,256,256]{4,3,2,1,0:T(8,128)(2,1)} %param.7), slice={[0:2], [1:12], [0:2], [0:256], [0:256]} | slice | bytes 11534336 | tf_op jit(solution)/shard_map/slice | solution.py:118
  5.8 0.0 slice-start
  5.8 4.6 %collective-permute-start = (bf16[2,11,2,256,256]{4,3,2,1,0:T(8,128)(2,1)}, bf16[2,11,2,256,256]{4,3,2,1,0:T(8,128)(2,1)}, u32[]{:S(2)}, u32[]{:S(2)}) collective-permute-start(bf16[2,11,2,256,256]{4,3,2,1,0:T(8,128)(2,1)} %slice.85), channel_id=1, source_target_pairs={{0,2},{2,4},{4,6},{6,8},{8,10},{10,12},{12,14},{14,16},{16,18},{18... | collective-permute-start | bytes 17301512 | tf_op jit(solution)/shard_map/ppermute | solution.py:41
  10.4 0.9 copy.37
  11.3 0.9 copy.36
  12.2 0.1 compare_select_fusion.2
  12.3 0.0 copy-done
  12.3 1.1 gather_fusion.1
  13.4 1.1 gather_fusion
  14.6 0.1 add_bitcast_fusion
  14.7 0.6 pad_maximum_fusion.1
  15.3 3.2 all-to-all-start
  18.5 0.8 multiply_reduce_fusion
  20.0 0.1 broadcast_multiply_fusion
  20.1 1.1 negate_convert_fusion
  21.2 53.8 %all-to-all-done = f32[2,1,128]{2,1,0:T(1,128)S(1)} async-done(((f32[2,1,128]{2,1,0:T(1,128)}), f32[2,1,128]{2,1,0:T(1,128)S(1)}, u32[]{:S(2)}, u32[]{:S(2)}) %all-to-all-start) | async-done | bytes 1056 | tf_op jit(solution)/shard_map/all_to_all | solution.py:26
  75.0 0.6 stack.56
  75.6 8.3 %all-to-all-start.1 = ((f32[8,2,128]{2,1,0:T(2,128)}), f32[8,2,128]{2,1,0:T(2,128)S(1)}, u32[]{:S(2)}, u32[]{:S(2)}) async-start(f32[8,2,128]{2,1,0:T(2,128)} %stack.56), calls=%async_computation.1 | async-start | bytes 16384 | tf_op jit(solution)/shard_map/all_to_all | solution.py:26
  83.9 1.0 fusion.16
  84.8 5.6 %all-to-all-done.1 = f32[8,2,128]{2,1,0:T(2,128)S(1)} async-done(((f32[8,2,128]{2,1,0:T(2,128)}), f32[8,2,128]{2,1,0:T(2,128)S(1)}, u32[]{:S(2)}, u32[]{:S(2)}) %all-to-all-start.1) | async-done | bytes 8224 | tf_op jit(solution)/shard_map/all_to_all | solution.py:26
  90.4 0.6 stack.57
  91.1 3.9 %all-to-all-start.2 = ((f32[4,16,128]{2,1,0:T(8,128)}), f32[4,16,128]{2,1,0:T(8,128)S(1)}, u32[]{:S(2)}, u32[]{:S(2)}) async-start(f32[4,16,128]{2,1,0:T(8,128)} %stack.57), calls=%async_computation.2 | async-start | bytes 65536 | tf_op jit(solution)/shard_map/all_to_all | solution.py:26
  95.0 4.3 %all-to-all-done.2 = f32[4,16,128]{2,1,0:T(8,128)S(1)} async-done(((f32[4,16,128]{2,1,0:T(8,128)}), f32[4,16,128]{2,1,0:T(8,128)S(1)}, u32[]{:S(2)}, u32[]{:S(2)}) %all-to-all-start.2) | async-done | bytes 32800 | tf_op jit(solution)/shard_map/all_to_all | solution.py:26
  99.2 0.6 pad_maximum_fusion
  99.9 3.3 all-to-all-start.3
  103.2 0.0 slice-start.1
  103.2 0.0 collective-permute-done
  103.2 5.9 %constant_dynamic-update-slice_fusion.1 = bf16[2,23,2,256,256]{4,3,2,1,0:T(8,128)(2,1)} fusion(bf16[2,11,2,256,256]{4,3,2,1,0:T(8,128)(2,1)} %collective-permute-done), kind=kLoop, calls=%fused_computation.84 | loop fusion | bytes 11534336
  109.1 0.0 slice-done
  109.1 0.0 slice-done.1
  109.1 3.1 constant_dynamic-update-slice_fusion
  112.2 31.7 %bitcast_convert_fusion = bf16[2,256,2,12,256]{4,1,3,2,0:T(8,128)(2,1)} fusion(bf16[2,12,2,256,256]{4,3,2,1,0:T(8,128)(2,1)S(1)} %bitcast.62, f32[256]{0:T(256)S(1)} %get-tuple-element.15, bf16[2,23,2,256,256]{4,3,2,1,0:T(8,128)(2,1)} %constant_dynamic-update-slice_fusion, f32[256]{0:T(256)S(1)} %get-tuple-element.16, f32[256]{0:T(256)S(1)} %get-tuple-element.17, ...), kind=kOutput, calls=%fused_computation.2 | convolution fusion | flops 3338665984 | bytes 82325504 | tf_op jit(solution)/shard_map/dot_general | solution.py:121
  143.9 0.0 copy-start.1
  143.9 12.8 %copy.32 = bf16[2,256,2,12,256]{4,0,3,2,1:T(2,128)(2,1)} copy(bf16[2,256,2,12,256]{4,1,3,2,0:T(8,128)(2,1)} %bitcast_convert_fusion) | data formatting | bytes 12582912 | tf_op jit(solution)/shard_map/reshape | solution.py:126
  156.7 0.0 all-to-all-done.3
  156.7 6.7 %all-to-all-start.4 = ((bf16[2,128,2,2,12,256]{5,0,4,3,2,1:T(2,128)(2,1)}), bf16[2,128,2,2,12,256]{5,0,4,3,2,1:T(2,128)(2,1)}, u32[]{:S(2)}, u32[]{:S(2)}) async-start(bf16[2,128,2,2,12,256]{5,0,4,3,2,1:T(2,128)(2,1)} %bitcast.60), calls=%async_computation.4 | async-start | bytes 12582912 | tf_op jit(solution)/shard_map/all_to_all | solution.py:129
  163.4 0.0 copy-done.1
  163.4 0.1 compare_select_fusion
  163.5 0.1 copy.18
  163.6 0.5 fusion.18
  164.1 0.5 fusion.57
  164.6 136.6 %all-to-all-done.4 = bf16[2,128,2,2,12,256]{5,0,4,3,2,1:T(2,128)(2,1)} async-done(((bf16[2,128,2,2,12,256]{5,0,4,3,2,1:T(2,128)(2,1)}), bf16[2,128,2,2,12,256]{5,0,4,3,2,1:T(2,128)(2,1)}, u32[]{:S(2)}, u32[]{:S(2)}) %all-to-all-start.4) | async-done | bytes 6291488 | tf_op jit(solution)/shard_map/all_to_all | solution.py:129
  301.3 10.0 %fusion = f32[2,2,64,128,2,12,1]{3,2,6,5,4,1,0:T(8,128)S(1)} fusion(bf16[2,128,2,2,12,256,1]{5,0,4,3,2,1,6:T(2,128)(2,1)} %bitcast.20, bf16[2,1,64,2,256]{4,2,3,1,0:T(8,128)(2,1)S(1)} %get-tuple-element.11, bf16[2,1,64,2,256]{4,2,3,1,0:T(8,128)(2,1)S(1)} %get-tuple-element.10), kind=kOutput, calls=%fused_computation.4 | convolution fusion | flops 805830656 | bytes 9699328 | tf_op jit(solution)/shard_map/dot_general | solution.py:127
  311.3 0.4 copy.43
  311.7 39.0 %all_to_all.30 = f32[2,2,2,32,128,2,12]{4,3,6,5,2,1,0:T(8,128)S(1)} all-to-all(f32[2,2,2,32,128,2,12]{4,3,6,5,2,1,0:T(8,128)S(1)} %bitcast.63), channel_id=1, replica_groups=mesh['chan_0'=8,'chan_1'=4,'chan_2'=2,'chan_3'=2,'stn'=2] {'stn'}, dimensions={0} | all-to-all | bytes 6291456 | tf_op jit(solution)/shard_map/all_to_all | solution.py:52
  350.7 1.4 reduce_sum.19
  352.1 6.6 %copy.25 = bf16[2,32,2,2,128,12]{1,3,5,4,2,0:T(2,128)(2,1)S(1)} copy(bf16[2,32,2,2,128,12]{4,1,5,2,0,3:T(8,128)(2,1)} %bitcast.66) | data formatting | bytes 1572864 | tf_op jit(solution)/shard_map/convert_element_type | solution.py:133
  358.8 5.0 %copy.26 = bf16[2,32,2,2,1536]{4,3,2,1,0:T(2,128)(2,1)} copy(bf16[2,32,2,2,1536]{1,3,4,2,0:T(2,128)(2,1)S(1)} %bitcast.65) | data formatting | bytes 1572864 | tf_op jit(solution)/shard_map/reshape | solution.py:135
  (8 shorter events, 0.1 us)
Async XLA Ops:
  0.0 12.3 %copy-start = (f32[4096]{0:T(1024)S(1)}, f32[4096]{0:T(1024)}, u32[]{:S(2)}) copy-start(f32[4096]{0:T(1024)} %param.8) | copy-start | bytes 49156
  5.8 103.3 %slice-start = ((s8[6291456]{0:T(1024)(128)(4,1)}), s8[2097152]{0:T(1024)(128)(4,1)S(1)}, s32[]{:S(2)}) async-start(s8[6291456]{0:T(1024)(128)(4,1)} %bitcast.61), calls=%async_computation.6 | async-start | bytes 4194304
  5.8 97.4 %collective-permute-start = (bf16[2,11,2,256,256]{4,3,2,1,0:T(8,128)(2,1)}, bf16[2,11,2,256,256]{4,3,2,1,0:T(8,128)(2,1)}, u32[]{:S(2)}, u32[]{:S(2)}) collective-permute-start(bf16[2,11,2,256,256]{4,3,2,1,0:T(8,128)(2,1)} %slice.85), channel_id=1, source_target_pairs={{0,2},{2,4},{4,6},{6,8},{8,10},{10,12},{12,14},{14,16},{16,18},{18... | collective-permute-start | bytes 17301512 | tf_op jit(solution)/shard_map/ppermute | solution.py:41
  15.3 59.7 %all-to-all-start = ((f32[2,1,128]{2,1,0:T(1,128)}), f32[2,1,128]{2,1,0:T(1,128)S(1)}, u32[]{:S(2)}, u32[]{:S(2)}) async-start(f32[2,1,128]{2,1,0:T(1,128)} %pad_maximum_fusion.1), calls=%async_computation | async-start | bytes 2048 | tf_op jit(solution)/shard_map/all_to_all | solution.py:26
  75.6 14.9 %all-to-all-start.1 = ((f32[8,2,128]{2,1,0:T(2,128)}), f32[8,2,128]{2,1,0:T(2,128)S(1)}, u32[]{:S(2)}, u32[]{:S(2)}) async-start(f32[8,2,128]{2,1,0:T(2,128)} %stack.56), calls=%async_computation.1 | async-start | bytes 16384 | tf_op jit(solution)/shard_map/all_to_all | solution.py:26
  91.1 8.2 %all-to-all-start.2 = ((f32[4,16,128]{2,1,0:T(8,128)}), f32[4,16,128]{2,1,0:T(8,128)S(1)}, u32[]{:S(2)}, u32[]{:S(2)}) async-start(f32[4,16,128]{2,1,0:T(8,128)} %stack.57), calls=%async_computation.2 | async-start | bytes 65536 | tf_op jit(solution)/shard_map/all_to_all | solution.py:26
  99.9 56.8 %all-to-all-start.3 = ((f32[2,64,128]{2,1,0:T(8,128)}), f32[2,64,128]{2,1,0:T(8,128)S(1)}, u32[]{:S(2)}, u32[]{:S(2)}) async-start(f32[2,64,128]{2,1,0:T(8,128)} %pad_maximum_fusion), calls=%async_computation.3 | async-start | bytes 131072 | tf_op jit(solution)/shard_map/all_to_all | solution.py:26
  103.2 5.9 %slice-start.1 = ((s8[6291456]{0:T(1024)(128)(4,1)}), s8[4194304]{0:T(1024)(128)(4,1)S(1)}, s32[]{:S(2)}) async-start(s8[6291456]{0:T(1024)(128)(4,1)} %bitcast.61), calls=%async_computation.7 | async-start | bytes 8388608
  143.9 19.5 %copy-start.1 = (s32[256]{0:T(256)S(1)}, s32[256]{0:T(256)}, u32[]{:S(2)}) copy-start(s32[256]{0:T(256)} %param.11) | copy-start | bytes 3076
  156.7 144.6 %all-to-all-start.4 = ((bf16[2,128,2,2,12,256]{5,0,4,3,2,1:T(2,128)(2,1)}), bf16[2,128,2,2,12,256]{5,0,4,3,2,1:T(2,128)(2,1)}, u32[]{:S(2)}, u32[]{:S(2)}) async-start(bf16[2,128,2,2,12,256]{5,0,4,3,2,1:T(2,128)(2,1)} %bitcast.60), calls=%async_computation.4 | async-start | bytes 12582912 | tf_op jit(solution)/shard_map/all_to_all | solution.py:129
